TPU v7x, 32 devices: a whole 2x2x4 slice. The times are simulated.
32 devices in a mesh: groups: 2 (over x), pool: 8 (over z, y), head: 2 (over core).
Axes of the slice: x: 2, y: 2, z: 4, core: 2. Of those that a mesh axis runs over, the one named last changes fastest.
Arguments:
- queries: bfloat16 [2048, 32, 128], P(('groups', 'pool'), 'head'), parts along dimension 0, may hold values from -400 to 400
- new_kv: bfloat16 [2048, 2, 4, 128], P(('groups', 'pool'), None, 'head'), parts along dimension 0, may hold values from -4 to 4
- pool: bfloat16 [528, 2, 4, 128, 128], P(('groups', 'pool'), None, 'head'), parts along dimension 0, may hold values from -6 to 6
- block_table: int32 [8, 64], P('groups'), parts along dimension 0, may hold values from -1 to 263, as said below
- prefix_len: int32 [8], P('groups'), parts along dimension 0, may hold values from 2048 to 8192, as said below
- new_slots: int32 [16], P('groups'), parts along dimension 0, may hold values from 0 to 263, as said below
Outputs:
- attended: bfloat16 [2048, 32, 128], P(('groups', 'pool'), 'head'), parts along dimension 0
- updated_pool: bfloat16 [528, 2, 4, 128, 128], P(('groups', 'pool'), None, 'head'), parts along dimension 0
There are 2 independent parts, one for each index of `groups`. A program takes and returns all parts, laid end to end along the dimension named above; each array names one. Nothing has to cross between parts.
Inputs may be any that keep to these rules, and one draw needn't show every extreme that they name: `block_table`: entry [r, j] is the slot (owner times 33 plus local slot) of page j of request r for j < ceil(prefix_len[r] / 128), and -1 after. All named slots differ. No owner holds more than 8 pages of one request, and the request with the longest prefix has exactly 8 on every owner. `prefix_len`: the longest prefix is exactly 8192 tokens. `new_slots`: entry d is a slot of owner d (d * 33 to (d + 1) * 33 - 1) that block_table does not name.
All inputs are finite; a program needn't handle non-finite values.
Results may differ from a plain program's by a relative error of at most 0.012.
Values may be sent and summed in bfloat16 or wider, within the bound.
No kernel may reach another device: no remote copies, remote signals or barrier semaphores. Data moves between devices by JAX's collectives and lax.ppermute only.
A program may use at most 128 MiB of HBM per device.

v0:
```python
import jax
import jax.numpy as jnp
from jax import lax
from jax.sharding import PartitionSpec as P

neg_big = -1e30
pages_per_step = 8


def swapped(array, axis, apart):
    return lax.ppermute(array, axis, [(i, i ^ 1 << apart) for i in range(lax.axis_size(axis))])


def select_pages(block_rows, lengths, holder, first_rank, take_count, slot_count, page_len):
    column = jnp.arange(block_rows.shape[1], dtype=jnp.int32)
    page_count = (lengths + page_len - 1) // page_len
    owned = (
        (block_rows // slot_count == holder[:, None])
        & (column[None, :] < page_count[:, None])
        & (block_rows >= 0)
    )
    order_rank = jnp.cumsum(owned.astype(jnp.int32), axis=1) - 1
    wanted = first_rank[:, None] + jnp.arange(take_count, dtype=jnp.int32)[None, :]
    matched = owned[:, None, :] & (order_rank[:, None, :] == wanted[:, :, None])
    present = jnp.any(matched, axis=-1)
    chosen = jnp.sum(jnp.where(matched, column[None, None, :], 0), axis=-1)
    slot_id = jnp.sum(jnp.where(matched, (block_rows % slot_count)[:, None, :], 0), axis=-1)
    return (chosen, slot_id, present)


def prepare(
    pool, block_table, prefix_len, owner_id, request_id, take_count, send_first, recv_first
):
    owner_count = lax.axis_size("pool")
    slot_count = pool.shape[0]
    page_len = pool.shape[3]
    targets = jnp.arange(owner_count, dtype=jnp.int32)
    send_rows = block_table[targets // 2]
    send_lengths = prefix_len[targets // 2]
    holder_self = jnp.full((owner_count,), owner_id, jnp.int32)
    unused, send_slots, unused_present = select_pages(
        send_rows, send_lengths, holder_self, send_first, take_count, slot_count, page_len
    )
    buffer = pool[send_slots]
    recv_rows = jnp.broadcast_to(block_table[request_id][None, :], send_rows.shape)
    recv_lengths = jnp.broadcast_to(prefix_len[request_id], (owner_count,))
    chosen, unused_slots, present = select_pages(
        recv_rows, recv_lengths, targets, recv_first, take_count, slot_count, page_len
    )
    position = chosen[..., None] * page_len + jnp.arange(page_len, dtype=jnp.int32)
    mask_in = (present[..., None] & (position < prefix_len[request_id])).reshape(-1, page_len)
    return (buffer, mask_in)


def update(running, scores, allowed, carry_values):
    top_old, total_old, acc_old = running
    scores = jnp.where(allowed, scores, neg_big)
    top_new = jnp.maximum(top_old, jnp.max(scores, axis=-1))
    weights = jnp.where(allowed, jnp.exp(scores - top_new[..., None]), 0.0)
    factor = jnp.exp(top_old - top_new)
    total_new = total_old * factor + jnp.sum(weights, axis=-1)
    acc_new = acc_old * factor[..., None] + carry_values(weights.astype(jnp.bfloat16))
    return (top_new, total_new, acc_new)


def attend(query_rows, pages_in, mask_in, recent_kv, recent_allowed, kv_heads, group_size):
    n_rows = query_rows.shape[0]
    head_dim = query_rows.shape[2]
    page_len = pages_in.shape[-2]
    scale = head_dim ** (-0.5)
    query_heads = query_rows.reshape(n_rows, kv_heads, group_size, head_dim)
    running = (
        jnp.full((kv_heads, group_size, n_rows), neg_big, jnp.float32),
        jnp.zeros((kv_heads, group_size, n_rows), jnp.float32),
        jnp.zeros((kv_heads, group_size, n_rows, head_dim), jnp.float32),
    )
    recent_scores = (
        jnp.einsum(
            "tkgd,ckd->kgtc", query_heads, recent_kv[:, 0], preferred_element_type=jnp.float32
        )
        * scale
    )

    def recent_values(probs):
        return jnp.einsum(
            "kgtc,ckd->kgtd", probs, recent_kv[:, 1], preferred_element_type=jnp.float32
        )

    running = update(running, recent_scores, recent_allowed[None, None], recent_values)

    def turn(turn_index, running):
        begin = turn_index * pages_per_step
        page_block = lax.dynamic_slice_in_dim(pages_in, begin, pages_per_step, 0)
        block_mask = lax.dynamic_slice_in_dim(mask_in, begin, pages_per_step, 0)
        scores = jnp.einsum(
            "tkgd,nkpd->kgtnp", query_heads, page_block[:, 0], preferred_element_type=jnp.float32
        )
        scores = scores.reshape(kv_heads, group_size, n_rows, pages_per_step * page_len) * scale

        def carry_values(probs):
            shaped = probs.reshape(kv_heads, group_size, n_rows, pages_per_step, page_len)
            return jnp.einsum(
                "kgtnp,nkpd->kgtd", shaped, page_block[:, 1], preferred_element_type=jnp.float32
            )

        return update(running, scores, block_mask.reshape(1, 1, 1, -1), carry_values)

    return lax.fori_loop(0, pages_in.shape[0] // pages_per_step, turn, running)


def half_of(device_ids):
    return 1 - (device_ids % 2 ^ device_ids // 2 % 2)


def on_device(queries, new_kv, pool, block_table, prefix_len, new_slots):
    owner_count = lax.axis_size("pool")
    owner_id = lax.axis_index("pool")
    request_id = owner_id // 2
    pair_half = half_of(owner_id)
    slot_count = pool.shape[0]
    kv_heads = pool.shape[2]
    page_len = pool.shape[3]
    head_dim = pool.shape[4]
    tok_rows = queries.shape[0]
    q_heads = queries.shape[1]
    group_size = q_heads // kv_heads
    page_cap = block_table.shape[1] // owner_count
    targets = jnp.arange(owner_count, dtype=jnp.int32)
    recent_pos = jnp.arange(2 * tok_rows, dtype=jnp.int32)
    half_cap = page_cap // 2
    send_first = half_of(targets) * half_cap
    recv_first = jnp.full((owner_count,), pair_half * half_cap, jnp.int32)
    buffer, mask_in = prepare(
        pool, block_table, prefix_len, owner_id, request_id, half_cap, send_first, recv_first
    )
    pages_in = lax.all_to_all(buffer, "pool", split_axis=0, concat_axis=0, tiled=True)
    pages_in = pages_in.reshape(-1, 2, kv_heads, page_len, head_dim)
    partner_q, partner = swapped((queries, new_kv), "pool", 0)
    recent_kv = jnp.where(
        pair_half == 0,
        jnp.concatenate([new_kv, partner], axis=0),
        jnp.concatenate([partner, new_kv], axis=0),
    )
    query_rows = jnp.where(
        pair_half == 0,
        jnp.concatenate([queries, partner_q], axis=0),
        jnp.concatenate([partner_q, queries], axis=0),
    )
    recent_allowed = (recent_pos[None, :] <= recent_pos[:, None]) & (pair_half == 0)
    running = attend(query_rows, pages_in, mask_in, recent_kv, recent_allowed, kv_heads, group_size)
    own_start = pair_half * tok_rows
    other_start = (1 - pair_half) * tok_rows
    own_part = tuple((lax.dynamic_slice_in_dim(piece, own_start, tok_rows, 2) for piece in running))
    theirs = tuple((lax.dynamic_slice_in_dim(piece, other_start, tok_rows, 2) for piece in running))
    returned = (
        swapped(theirs[0].astype(jnp.bfloat16), "pool", 0).astype(jnp.float32),
        swapped(theirs[1].astype(jnp.bfloat16), "pool", 0).astype(jnp.float32),
        swapped(theirs[2].astype(jnp.bfloat16), "pool", 0).astype(jnp.float32),
    )
    top_new = jnp.maximum(own_part[0], returned[0])
    factor_own = jnp.exp(own_part[0] - top_new)
    factor_back = jnp.exp(returned[0] - top_new)
    total_new = own_part[1] * factor_own + returned[1] * factor_back
    acc_new = own_part[2] * factor_own[..., None] + returned[2] * factor_back[..., None]
    combined = (top_new, total_new, acc_new)
    mixed = combined[2] / combined[1][..., None]
    attended = mixed.transpose(2, 0, 1, 3).reshape(tok_rows, q_heads, head_dim).astype(jnp.bfloat16)
    new_page = new_kv.transpose(1, 2, 0, 3)[None]
    own_slot = lax.dynamic_index_in_dim(new_slots, owner_id, 0, keepdims=False)
    slot_id = own_slot % slot_count
    updated_pool = lax.dynamic_update_slice_in_dim(pool, new_page, slot_id, 0)
    return (attended, updated_pool)


def solution(mesh):
    placed = (
        P(("groups", "pool"), "head", None),
        P(("groups", "pool"), None, "head", None),
        P(("groups", "pool"), None, "head", None, None),
        P("groups", None),
        P("groups"),
        P("groups"),
    )
    return jax.shard_map(
        on_device,
        mesh=mesh,
        in_specs=placed,
        out_specs=(
            P(("groups", "pool"), "head", None),
            P(("groups", "pool"), None, "head", None, None),
        ),
        check_vma=False,
    )
```

profile of v0, /device:TPU:0, one launch (start us, length us, event | category | flops | bytes accessed | tf_op | source)
XLA Modules:
  0.0 199.8 jit_solution(16582899362481627354)
XLA Ops:
  0.7 5.9 %copy.109 = bf16[33,2,2,128,128]{4,3,2,1,0:T(8,128)(2,1)} copy(bf16[33,2,2,128,128]{4,3,2,1,0:T(8,128)(2,1)} %param.10) | data formatting | bytes 8650752
  6.6 0.6 gather_fusion.1
  7.3 0.6 gather_fusion
  7.9 0.2 reduce_window_sum.18
  8.2 0.2 select_reduce_fusion
  8.6 5.2 %gather_fusion.2 = bf16[32,2,2,128,128]{4,3,2,1,0:T(8,128)(2,1)} fusion(bf16[33,2,2,128,128]{4,3,2,1,0:T(8,128)(2,1)} %copy.109, s32[1024]{0:T(1024)S(1)} %pad_clamp_fusion), kind=kCustom, calls=%fused_computation.2 | custom fusion | bytes 8388736 | tf_op jit(solution)/shard_map/gather | solution.py:44
  13.8 4.7 %copy.63 = bf16[8,4,2,2,128,128]{5,4,1,3,2,0:T(8,128)(2,1)} copy(bf16[8,4,2,2,128,128]{5,4,3,2,1,0:T(8,128)(2,1)} %bitcast.113) | data formatting | bytes 8388608 | tf_op jit(solution)/shard_map/gather | solution.py:44
  18.6 7.4 %all-to-all-start = ((bf16[8,4,2,2,128,128]{5,4,1,3,2,0:T(8,128)(2,1)}), bf16[8,4,2,2,128,128]{5,4,1,3,2,0:T(8,128)(2,1)}, u32[]{:S(2)}, u32[]{:S(2)}) async-start(bf16[8,4,2,2,128,128]{5,4,1,3,2,0:T(8,128)(2,1)} %copy.63), calls=%async_computation | async-start | bytes 8388608 | tf_op jit(solution)/shard_map/all_to_all | solution.py:136
  26.0 2.1 %collective-permute-start = (bf16[128,2,2,128]{3,0,2,1:T(8,128)(2,1)S(1)}, bf16[128,2,2,128]{3,0,2,1:T(8,128)(2,1)S(1)}, u32[]{:S(2)}, u32[]{:S(2)}) collective-permute-start(bf16[128,2,2,128]{3,0,2,1:T(8,128)(2,1)S(1)} %copy.55), channel_id=1, source_target_pairs={{0,2},{2,0},{4,6},{6,4},{8,10},{10,8},{12,14},{14,12},{1,3},{3,1},... | collective-permute-start | bytes 393224 | tf_op jit(solution)/shard_map/ppermute | solution.py:11
  28.2 0.6 dynamic_slice.44
  29.5 0.2 reduce_window_sum.17
  29.8 0.2 select_reduce_fusion.1
  30.0 0.2 fusion.34
  30.6 0.7 fusion.33
  31.3 0.6 dynamic_slice.51
  32.4 0.1 copy.57
  32.6 32.2 %collective-permute-done = bf16[128,2,2,128]{3,0,2,1:T(8,128)(2,1)S(1)} collective-permute-done((bf16[128,2,2,128]{3,0,2,1:T(8,128)(2,1)S(1)}, bf16[128,2,2,128]{3,0,2,1:T(8,128)(2,1)S(1)}, u32[]{:S(2)}, u32[]{:S(2)}) %collective-permute-start) | collective-permute-done | bytes 131104 | tf_op jit(solution)/shard_map/ppermute | solution.py:11
  65.0 12.5 %collective-permute-done.1 = bf16[128,16,128]{2,1,0:T(8,128)(2,1)S(1)} collective-permute-done((bf16[128,16,128]{2,1,0:T(8,128)(2,1)S(1)}, bf16[128,16,128]{2,1,0:T(8,128)(2,1)S(1)}, u32[]{:S(2)}, u32[]{:S(2)}) %collective-permute-start.1) | collective-permute-done | bytes 524320 | tf_op jit(solution)/shard_map/ppermute | solution.py:11
  77.6 0.3 maximum_select_fusion
  77.9 0.8 fusion.17
  78.6 1.0 fusion.19
  79.7 1.7 fusion.27
  81.4 37.9 %all-to-all-done = bf16[8,4,2,2,128,128]{5,4,1,3,2,0:T(8,128)(2,1)} async-done(((bf16[8,4,2,2,128,128]{5,4,1,3,2,0:T(8,128)(2,1)}), bf16[8,4,2,2,128,128]{5,4,1,3,2,0:T(8,128)(2,1)}, u32[]{:S(2)}, u32[]{:S(2)}) %all-to-all-start) | async-done | bytes 4194336 | tf_op jit(solution)/shard_map/all_to_all | solution.py:136
  119.3 4.7 %copy.64 = bf16[8,4,2,2,128,128]{5,4,3,2,1,0:T(8,128)(2,1)} copy(bf16[8,4,2,2,128,128]{5,4,1,3,2,0:T(8,128)(2,1)} %all-to-all-done) | data formatting | bytes 8388608 | tf_op jit(solution)/shard_map/all_to_all | solution.py:136
  124.0 59.1 %while.17 = (s32[]{:T(128)}, f32[2,8,256]{2,1,0:T(8,128)S(1)}, f32[2,8,256]{2,1,0:T(8,128)S(1)}, f32[2,8,256,128]{3,2,1,0:T(8,128)S(1)}, pred[32,128]{1,0:T(8,12...) while((s32[]{:T(128)}, f32[2,8,256]{2,1,0:T(8,128)S(1)}, ...), condition=%wide.region_10.11_spmd, body=%wide.region_7.10_spmd.sunk | while | flops 2203066368 | bytes 58987704 | solution.py:108
  124.0 1.3 constant_dynamic-slice_fusion.7
  125.3 2.5 %bitcast_reduce_fusion.2 = (f32[2,8,256]{2,1,0:T(8,128)S(1)}, f32[2,8,128,256,8]{3,2,4,1,0:T(8,128)S(1)}) fusion(pred[8,128]{1,0:T(8,128)(4,1)S(1)} %constant_dynamic-slice_fusion.6, bf16[256,2,8,128]{3,0,2,1:T(8,128)(2,1)S(1)} %get-tuple-element.267, bf16[8,1,2,128,128]{4,3,2,1,0:T(8,128)(2,1)S(1)} %get-tuple-element.231), kind=kOutput, calls=%fused_computation.4.clone.1 | convolution fusion | flops 1086320640 | bytes 18367488 | tf_op jit(solution)/shard_map/while/body/eval_jaxpr/tkgd,nkpd->kgtnp/dot_general | solution.py:95
  127.9 4.4 %fusion.64 = f32[2,8,256]{2,1,0:T(8,128)S(1)} fusion(f32[2,8,128,256,8]{3,2,4,1,0:T(8,128)S(1)} %get-tuple-element.233, f32[2,8,256]{2,1,0:T(8,128)S(1)} %max.20, pred[8,128]{1,0:T(8,128)(4,1)S(1)} %constant_dynamic-slice_fusion.6), kind=kLoop, calls=%fused_computation.9.clone.1 | loop fusion | flops 20967424 | bytes 16811008 | tf_op jit(solution)/shard_map/while/body/eval_jaxpr/reduce_sum | solution.py:61
  132.3 6.4 %bitcast_add_fusion.2 = f32[2,8,256,128]{3,2,1,0:T(8,128)S(1)} fusion(f32[2,8,256,128]{3,2,1,0:T(8,128)S(1)} %get-tuple-element.252, f32[2,8,128,256,8]{3,2,4,1,0:T(8,128)S(1)} %get-tuple-element.233, f32[2,8,256]{2,1,0:T(8,128)S(1)} %max.20, pred[8,128]{1,0:T(8,128)(4,1)S(1)} %constant_dynamic-slice_fusion.6, ...), kind=kOutput, calls=%fused_computation.13.clone.1 | convolution fusion | flops 1095761920 | bytes 21529600 | tf_op jit(solution)/shard_map/while/body/eval_jaxpr/kgtnp,nkpd->kgtd/dot_general | solution.py:102
  138.8 1.3 constant_dynamic-slice_fusion.7
  140.1 2.5 %bitcast_reduce_fusion.2 = (f32[2,8,256]{2,1,0:T(8,128)S(1)}, f32[2,8,128,256,8]{3,2,4,1,0:T(8,128)S(1)}) fusion(pred[8,128]{1,0:T(8,128)(4,1)S(1)} %constant_dynamic-slice_fusion.6, bf16[256,2,8,128]{3,0,2,1:T(8,128)(2,1)S(1)} %get-tuple-element.267, bf16[8,1,2,128,128]{4,3,2,1,0:T(8,128)(2,1)S(1)} %get-tuple-element.231), kind=kOutput, calls=%fused_computation.4.clone.1 | convolution fusion | flops 1086320640 | bytes 18367488 | tf_op jit(solution)/shard_map/while/body/eval_jaxpr/tkgd,nkpd->kgtnp/dot_general | solution.py:95
  142.7 4.4 %fusion.64 = f32[2,8,256]{2,1,0:T(8,128)S(1)} fusion(f32[2,8,128,256,8]{3,2,4,1,0:T(8,128)S(1)} %get-tuple-element.233, f32[2,8,256]{2,1,0:T(8,128)S(1)} %max.20, pred[8,128]{1,0:T(8,128)(4,1)S(1)} %constant_dynamic-slice_fusion.6), kind=kLoop, calls=%fused_computation.9.clone.1 | loop fusion | flops 20967424 | bytes 16811008 | tf_op jit(solution)/shard_map/while/body/eval_jaxpr/reduce_sum | solution.py:61
  147.1 6.4 %bitcast_add_fusion.2 = f32[2,8,256,128]{3,2,1,0:T(8,128)S(1)} fusion(f32[2,8,256,128]{3,2,1,0:T(8,128)S(1)} %get-tuple-element.252, f32[2,8,128,256,8]{3,2,4,1,0:T(8,128)S(1)} %get-tuple-element.233, f32[2,8,256]{2,1,0:T(8,128)S(1)} %max.20, pred[8,128]{1,0:T(8,128)(4,1)S(1)} %constant_dynamic-slice_fusion.6, ...), kind=kOutput, calls=%fused_computation.13.clone.1 | convolution fusion | flops 1095761920 | bytes 21529600 | tf_op jit(solution)/shard_map/while/body/eval_jaxpr/kgtnp,nkpd->kgtd/dot_general | solution.py:102
  153.6 1.3 constant_dynamic-slice_fusion.7
  154.9 2.5 %bitcast_reduce_fusion.2 = (f32[2,8,256]{2,1,0:T(8,128)S(1)}, f32[2,8,128,256,8]{3,2,4,1,0:T(8,128)S(1)}) fusion(pred[8,128]{1,0:T(8,128)(4,1)S(1)} %constant_dynamic-slice_fusion.6, bf16[256,2,8,128]{3,0,2,1:T(8,128)(2,1)S(1)} %get-tuple-element.267, bf16[8,1,2,128,128]{4,3,2,1,0:T(8,128)(2,1)S(1)} %get-tuple-element.231), kind=kOutput, calls=%fused_computation.4.clone.1 | convolution fusion | flops 1086320640 | bytes 18367488 | tf_op jit(solution)/shard_map/while/body/eval_jaxpr/tkgd,nkpd->kgtnp/dot_general | solution.py:95
  157.5 4.4 %fusion.64 = f32[2,8,256]{2,1,0:T(8,128)S(1)} fusion(f32[2,8,128,256,8]{3,2,4,1,0:T(8,128)S(1)} %get-tuple-element.233, f32[2,8,256]{2,1,0:T(8,128)S(1)} %max.20, pred[8,128]{1,0:T(8,128)(4,1)S(1)} %constant_dynamic-slice_fusion.6), kind=kLoop, calls=%fused_computation.9.clone.1 | loop fusion | flops 20967424 | bytes 16811008 | tf_op jit(solution)/shard_map/while/body/eval_jaxpr/reduce_sum | solution.py:61
  161.9 6.4 %bitcast_add_fusion.2 = f32[2,8,256,128]{3,2,1,0:T(8,128)S(1)} fusion(f32[2,8,256,128]{3,2,1,0:T(8,128)S(1)} %get-tuple-element.252, f32[2,8,128,256,8]{3,2,4,1,0:T(8,128)S(1)} %get-tuple-element.233, f32[2,8,256]{2,1,0:T(8,128)S(1)} %max.20, pred[8,128]{1,0:T(8,128)(4,1)S(1)} %constant_dynamic-slice_fusion.6, ...), kind=kOutput, calls=%fused_computation.13.clone.1 | convolution fusion | flops 1095761920 | bytes 21529600 | tf_op jit(solution)/shard_map/while/body/eval_jaxpr/kgtnp,nkpd->kgtd/dot_general | solution.py:102
  168.4 1.3 constant_dynamic-slice_fusion.7
  169.7 2.5 %bitcast_reduce_fusion.2 = (f32[2,8,256]{2,1,0:T(8,128)S(1)}, f32[2,8,128,256,8]{3,2,4,1,0:T(8,128)S(1)}) fusion(pred[8,128]{1,0:T(8,128)(4,1)S(1)} %constant_dynamic-slice_fusion.6, bf16[256,2,8,128]{3,0,2,1:T(8,128)(2,1)S(1)} %get-tuple-element.267, bf16[8,1,2,128,128]{4,3,2,1,0:T(8,128)(2,1)S(1)} %get-tuple-element.231), kind=kOutput, calls=%fused_computation.4.clone.1 | convolution fusion | flops 1086320640 | bytes 18367488 | tf_op jit(solution)/shard_map/while/body/eval_jaxpr/tkgd,nkpd->kgtnp/dot_general | solution.py:95
  172.2 4.4 %fusion.64 = f32[2,8,256]{2,1,0:T(8,128)S(1)} fusion(f32[2,8,128,256,8]{3,2,4,1,0:T(8,128)S(1)} %get-tuple-element.233, f32[2,8,256]{2,1,0:T(8,128)S(1)} %max.20, pred[8,128]{1,0:T(8,128)(4,1)S(1)} %constant_dynamic-slice_fusion.6), kind=kLoop, calls=%fused_computation.9.clone.1 | loop fusion | flops 20967424 | bytes 16811008 | tf_op jit(solution)/shard_map/while/body/eval_jaxpr/reduce_sum | solution.py:61
  176.7 6.4 %bitcast_add_fusion.2 = f32[2,8,256,128]{3,2,1,0:T(8,128)S(1)} fusion(f32[2,8,256,128]{3,2,1,0:T(8,128)S(1)} %get-tuple-element.252, f32[2,8,128,256,8]{3,2,4,1,0:T(8,128)S(1)} %get-tuple-element.233, f32[2,8,256]{2,1,0:T(8,128)S(1)} %max.20, pred[8,128]{1,0:T(8,128)(4,1)S(1)} %constant_dynamic-slice_fusion.6, ...), kind=kOutput, calls=%fused_computation.13.clone.1 | convolution fusion | flops 1095761920 | bytes 21529600 | tf_op jit(solution)/shard_map/while/body/eval_jaxpr/kgtnp,nkpd->kgtd/dot_general | solution.py:102
  183.2 1.5 collective-permute-start.4
  184.8 0.6 collective-permute-start.3
  185.4 1.5 collective-permute-start.2
  186.9 0.7 bitcast_dynamic-update-slice_fusion
  187.6 10.1 %collective-permute-done.2 = bf16[2,8,128]{2,1,0:T(8,128)(2,1)S(1)} collective-permute-done((bf16[2,8,128]{2,1,0:T(8,128)(2,1)S(1)}, bf16[2,8,128]{2,1,0:T(8,128)(2,1)S(1)}, u32[]{:S(2)}, u32[]{:S(2)}) %collective-permute-start.2) | collective-permute-done | bytes 4128 | tf_op jit(solution)/shard_map/ppermute | solution.py:11
  197.7 1.0 fusion.30
  198.7 1.1 copy.90
  (60 shorter events, 1.3 us)
Async XLA Ops:
  0.6 6.6 %copy-start.1 = (s32[4,64]{1,0:T(4,128)S(1)}, s32[4,64]{1,0:T(4,128)}, u32[]{:S(2)}) copy-start(s32[4,64]{1,0:T(4,128)} %param.11) | copy-start | bytes 3076
  0.6 6.0 %copy-start = (s32[4]{0:T(128)S(1)}, s32[4]{0:T(128)}, u32[]{:S(2)}) copy-start(s32[4]{0:T(128)} %param.12) | copy-start | bytes 52
  18.5 7.5 %copy-start.3 = (bf16[128,2,2,128]{3,2,1,0:T(2,128)(2,1)S(1)}, bf16[128,2,2,128]{3,2,1,0:T(2,128)(2,1)}, u32[]{:S(2)}) copy-start(bf16[128,2,2,128]{3,2,1,0:T(2,128)(2,1)} %param.9) | copy-start | bytes 393220
  18.5 9.6 %copy-start.2 = (bf16[128,16,128]{2,1,0:T(8,128)(2,1)S(1)}, bf16[128,16,128]{2,1,0:T(8,128)(2,1)}, u32[]{:S(2)}) copy-start(bf16[128,16,128]{2,1,0:T(8,128)(2,1)} %param.8) | copy-start | bytes 1572868
  18.5 12.7 %copy-start.4 = (s32[8]{0:T(128)S(1)}, s32[8]{0:T(128)}, u32[]{:S(2)}) copy-start(s32[8]{0:T(128)} %param.13) | copy-start | bytes 100
  18.6 100.7 %all-to-all-start = ((bf16[8,4,2,2,128,128]{5,4,1,3,2,0:T(8,128)(2,1)}), bf16[8,4,2,2,128,128]{5,4,1,3,2,0:T(8,128)(2,1)}, u32[]{:S(2)}, u32[]{:S(2)}) async-start(bf16[8,4,2,2,128,128]{5,4,1,3,2,0:T(8,128)(2,1)} %copy.63), calls=%async_computation | async-start | bytes 8388608 | tf_op jit(solution)/shard_map/all_to_all | solution.py:136
  26.0 38.8 %collective-permute-start = (bf16[128,2,2,128]{3,0,2,1:T(8,128)(2,1)S(1)}, bf16[128,2,2,128]{3,0,2,1:T(8,128)(2,1)S(1)}, u32[]{:S(2)}, u32[]{:S(2)}) collective-permute-start(bf16[128,2,2,128]{3,0,2,1:T(8,128)(2,1)S(1)} %copy.55), channel_id=1, source_target_pairs={{0,2},{2,0},{4,6},{6,4},{8,10},{10,8},{12,14},{14,12},{1,3},{3,1},... | collective-permute-start | bytes 393224 | tf_op jit(solution)/shard_map/ppermute | solution.py:11
  28.1 49.3 %collective-permute-start.1 = (bf16[128,16,128]{2,1,0:T(8,128)(2,1)S(1)}, bf16[128,16,128]{2,1,0:T(8,128)(2,1)S(1)}, u32[]{:S(2)}, u32[]{:S(2)}) collective-permute-start(bf16[128,16,128]{2,1,0:T(8,128)(2,1)S(1)} %copy-done.2), channel_id=1, source_target_pairs={{0,2},{2,0},{4,6},{6,4},{8,10},{10,8},{12,14},{14,12},{1,3},{3,1},... | collective-permute-start | bytes 1572872 | tf_op jit(solution)/shard_map/ppermute | solution.py:11
  183.2 4.4 %collective-permute-start.4 = (bf16[2,8,128]{2,1,0:T(8,128)(2,1)S(1)}, bf16[2,8,128]{2,1,0:T(8,128)(2,1)S(1)}, u32[]{:S(2)}, u32[]{:S(2)}) collective-permute-start(bf16[2,8,128]{2,1,0:T(8,128)(2,1)S(1)} %dynamic-slice_convert_fusion.1), channel_id=1, source_target_pairs={{0,2},{2,0},{4,6},{6,4},{8,10},{10,8},{12,14},{14,12},{1,3},{3,1},... | collective-permute-start | bytes 12296 | tf_op jit(solution)/shard_map/ppermute | solution.py:11
  184.8 12.9 %collective-permute-start.3 = (bf16[2,8,128,128]{3,2,1,0:T(8,128)(2,1)S(1)}, bf16[2,8,128,128]{3,2,1,0:T(8,128)(2,1)S(1)}, u32[]{:S(2)}, u32[]{:S(2)}) collective-permute-start(bf16[2,8,128,128]{3,2,1,0:T(8,128)(2,1)S(1)} %dynamic-slice_convert_fusion), channel_id=1, source_target_pairs={{0,2},{2,0},{4,6},{6,4},{8,10},{10,8},{12,14},{14,12},{1,3},{3,1},... | collective-permute-start | bytes 1572872 | tf_op jit(solution)/shard_map/ppermute | solution.py:11
  185.4 12.2 %collective-permute-start.2 = (bf16[2,8,128]{2,1,0:T(8,128)(2,1)S(1)}, bf16[2,8,128]{2,1,0:T(8,128)(2,1)S(1)}, u32[]{:S(2)}, u32[]{:S(2)}) collective-permute-start(bf16[2,8,128]{2,1,0:T(8,128)(2,1)S(1)} %dynamic-slice_convert_fusion.2), channel_id=1, source_target_pairs={{0,2},{2,0},{4,6},{6,4},{8,10},{10,8},{12,14},{14,12},{1,3},{3,1},... | collective-permute-start | bytes 12296 | tf_op jit(solution)/shard_map/ppermute | solution.py:11
where the time goes:
time: 200 us
  waiting for transfers between devices  92.7 us (46%)
  matrix products  38.2 us (19%)
  local copies, waits for them, and re-layouts  31 us (16%)
  other arithmetic  22.3 us (11%)
  starting transfers between devices  13.2 us (7%)
  between operations  2.14 us (1%)
    ppermute x5, waiting for transfers between devices, swapped(): lax.ppermute(array, axis, [(i, i ^ 1 << apart) for i in range(lax.axis_si...  54.8 us
    all_to_all x1, waiting for transfers between devices, on_device(): lax.all_to_all(buffer, 'pool', split_axis=0, concat_axis=0, tiled=True)  37.9 us
    dot_general x4, matrix products, carry_values(): jnp.einsum('kgtnp,nkpd->kgtd', shaped, page_block[:, 1], preferred_elemen...  25.7 us
    reduce_sum x5, other arithmetic, update(): total_new = total_old * factor + jnp.sum(weights, axis=-1)  18.8 us
    dot_general x4, matrix products, turn(): jnp.einsum('tkgd,nkpd->kgtnp', query_heads, page_block[:, 0], preferred_e...  10.1 us
    gather x2, local copies, waits for them, and re-layouts, prepare(): buffer = pool[send_slots]  9.98 us
    all_to_all x1, starting transfers between devices, on_device(): lax.all_to_all(buffer, 'pool', split_axis=0, concat_axis=0, tiled=True)  7.44 us
    unnamed x13, local copies, waits for them, and re-layouts  6.1 us
  transfers between devices with their start and end apart: 6, of which 4 were waited for; matrix products, arithmetic and copies ran while one was open for 4% of the time, Pallas kernels for 0%

commit v1 on v0

v1 whole, which is shorter than its diff:
```python
import functools

import jax
import jax.numpy as jnp
from jax import lax
from jax.experimental import pallas as pl
from jax.experimental.pallas import tpu as pltpu
from jax.sharding import PartitionSpec as P

log2_e = 1.4426950408889634
hidden_score = -2e30
lowest_top = -1e30
lanes = 128
block_rows = 128


def moved(array, apart):
    count = lax.axis_size("pool")
    return lax.ppermute(array, "pool", [(i, i ^ apart) for i in range(count)])


def whole(array):
    return pl.BlockSpec(array.shape, lambda i, *_: (0,) * len(array.shape))


def diagonal():
    shape = (lanes, lanes)
    return lax.broadcasted_iota(jnp.int32, shape, 0) == lax.broadcasted_iota(jnp.int32, shape, 1)


def as_row(column, eye):
    spread = jnp.where(eye, jnp.broadcast_to(column, (lanes, lanes)), 0.0)
    return jnp.sum(spread, axis=0, keepdims=True)


def as_column(row, eye):
    spread = jnp.where(eye, jnp.broadcast_to(row, (lanes, lanes)), 0.0)
    return jnp.sum(spread, axis=1, keepdims=True)


def in_three(values):
    high = values.astype(jnp.bfloat16)
    rest = values - high.astype(jnp.float32)
    middle = rest.astype(jnp.bfloat16)
    low = (rest - middle.astype(jnp.float32)).astype(jnp.bfloat16)
    return (high, middle, low)


def from_three(ref, begin, count):
    parts = [
        ref[begin + i * count : begin + (i + 1) * count].astype(jnp.float32) for i in range(3)
    ]
    return parts[0] + parts[1] + parts[2]


def gather_body(owner_ref, table_ref, pool_ref, *refs, lists, kv_heads, cap):
    outs = refs[:-2]
    slots, sem = refs[-2:]
    owner = owner_ref[0]
    pair = owner // 2
    slot_count = pool_ref.shape[0]
    base = owner * slot_count
    width = table_ref.shape[1]
    copies = []
    for at, which in enumerate(lists):
        request = pair ^ which
        begin = at * (cap + 1)

        def look(j, found):
            slot = table_ref[request, j] - base
            slots[begin + jnp.minimum(found, cap)] = slot
            held = (slot >= 0) & (slot < slot_count)
            return found + held.astype(jnp.int32)

        found = lax.fori_loop(0, width, look, jnp.int32(0), unroll=8)
        for i in range(cap):
            slot = jnp.where(i < found, slots[begin + i], 0)
            for k in range(kv_heads):
                copy = pltpu.make_async_copy(
                    pool_ref.at[slot, :, k], outs[at * kv_heads + k].at[i], sem.at[at, k, i]
                )
                copy.start()
                copies.append(copy)
    for copy in copies:
        copy.wait()


def gather_pages(owner, table, pool, lists, cap):
    slot_count, pair_of, kv_heads, page_len, head_dim = pool.shape
    shape = jax.ShapeDtypeStruct((cap, pair_of, page_len, head_dim), pool.dtype)
    count = len(lists) * kv_heads
    outs = pl.pallas_call(
        functools.partial(gather_body, lists=lists, kv_heads=kv_heads, cap=cap),
        out_shape=[shape] * count,
        grid_spec=pltpu.PrefetchScalarGridSpec(
            num_scalar_prefetch=2,
            grid=(1,),
            in_specs=[pl.BlockSpec(memory_space=pl.ANY)],
            out_specs=[pl.BlockSpec(memory_space=pl.ANY)] * count,
            scratch_shapes=[
                pltpu.SMEM((len(lists) * (cap + 1),), jnp.int32),
                pltpu.SemaphoreType.DMA((len(lists), kv_heads, cap)),
            ],
        ),
        name="gather_pages",
    )(owner, table, pool)
    return [outs[i * kv_heads : (i + 1) * kv_heads] for i in range(len(lists))]


def attend_body(info_ref, *refs, halves, source_count, has_page, has_prev, packed, step_rows, group, scale, copies_pool):
    refs = list(refs)
    q_refs = [refs.pop(0) for _ in range(halves)]
    kv_refs = [refs.pop(0) for _ in range(source_count)]
    page_ref = refs.pop(0) if has_page else None
    prev_refs = [(refs.pop(0), refs.pop(0)) for _ in range(halves)] if has_prev else None
    pool_refs = [refs.pop(0) for _ in range(2)] if copies_pool else None
    out_refs = []
    for h in range(halves):
        out_refs.append((refs.pop(0),) if packed[h] else (refs.pop(0), refs.pop(0)))
    new_pool = refs.pop(0) if copies_pool else None
    wide_values = refs.pop(0)
    tables = [refs.pop(0) if packed[h] else out_refs[h][1] for h in range(halves)]
    sem = refs.pop(0) if copies_pool else None
    step = pl.program_id(0)
    steps = pl.num_programs(0)
    keys = [ref.shape[0] * ref.shape[2] for ref in kv_refs]
    page_len = kv_refs[0].shape[2]

    def pool_copy(slot, source):
        return pltpu.make_async_copy(source, new_pool.at[slot], sem)

    if copies_pool:

        @pl.when(step == 0)
        def _():
            fresh = info_ref[source_count + 1]

            def start(slot, carry):
                @pl.when(slot == fresh)
                def _():
                    pool_copy(slot, pool_refs[1]).start()

                @pl.when(slot != fresh)
                def _():
                    pool_copy(slot, pool_refs[0].at[slot]).start()

                return carry

            lax.fori_loop(0, new_pool.shape[0], start, 0)

    @pl.when(step == 0)
    def _():
        ones = jnp.ones((page_len, lanes), jnp.bfloat16)
        begin = 0
        for ref in kv_refs:
            for p in range(ref.shape[0]):
                wide_values[begin : begin + page_len, :lanes] = ref[p, 1]
                wide_values[begin : begin + page_len, lanes:] = ones
                begin += page_len
        if has_page:
            wide_values[begin : begin + page_len, :lanes] = page_ref[1]
            wide_values[begin : begin + page_len, lanes:] = ones

    eye = diagonal()
    limits = []
    for s in range(source_count):
        position = lax.broadcasted_iota(jnp.int32, (1, keys[s]), 1)
        limit = jnp.where(position < info_ref[s], jnp.inf, hidden_score)
        limits.append(limit.astype(jnp.float32))
    for h in range(halves):
        for t in range(step_rows // block_rows):
            rows = slice(t * block_rows, (t + 1) * block_rows)
            query = q_refs[h][rows]
            scores = []
            for s in range(source_count):
                key_rows = kv_refs[s][:, 0].reshape(keys[s], lanes)
                product = lax.dot_general(
                    query, key_rows, (((1,), (1,)), ((), ())), preferred_element_type=jnp.float32
                )
                scores.append(jnp.minimum(product, limits[s]))
            if has_page:
                product = lax.dot_general(
                    query, page_ref[0], (((1,), (1,)), ((), ())), preferred_element_type=jnp.float32
                )
                key_at = lax.broadcasted_iota(jnp.int32, product.shape, 1)
                if h == 0:
                    row_at = lax.broadcasted_iota(jnp.int32, product.shape, 0)
                    token = (step * step_rows + t * block_rows + row_at) // group
                    seen = key_at <= token
                else:
                    seen = key_at < info_ref[source_count]
                scores.append(jnp.where(seen, product, hidden_score))
            top = jnp.full((block_rows, 1), lowest_top, jnp.float32)
            for part in scores:
                top = jnp.maximum(top, jnp.max(part, axis=1, keepdims=True))
            scaled_top = top * scale
            mixed = None
            begin = 0
            for part in scores:
                weights = jnp.exp2(part * scale - scaled_top).astype(jnp.bfloat16)
                values = wide_values[begin : begin + part.shape[1]]
                begin += part.shape[1]
                product = jnp.dot(weights, values, preferred_element_type=jnp.float32)
                mixed = product if mixed is None else mixed + product
            total = mixed[:, lanes : lanes + 1]
            mixed = mixed[:, :lanes]
            row = step * (step_rows // block_rows) + t
            count = tables[h].shape[0] // 2
            if has_prev:
                prev_mixed, prev_table = prev_refs[h]
                prev_top = as_column(prev_table[pl.ds(row, 1)], eye)
                prev_total = as_column(prev_table[pl.ds(count + row, 1)], eye)
                joint = jnp.maximum(top, prev_top)
                keep = jnp.exp2((top - joint) * scale)
                keep_prev = jnp.exp2((prev_top - joint) * scale)
                mixed = mixed * keep + prev_mixed[rows] * keep_prev
                total = total * keep + prev_total * keep_prev
                top = joint
            tables[h][pl.ds(row, 1)] = as_row(top, eye)
            tables[h][pl.ds(count + row, 1)] = as_row(total, eye)
            if packed[h]:
                at = pl.multiple_of(row * block_rows, block_rows)
                out_refs[h][0][pl.ds(at, block_rows)] = mixed.astype(jnp.bfloat16)
            else:
                out_refs[h][0][rows] = mixed

    @pl.when(step == steps - 1)
    def _():
        for h in range(halves):
            if packed[h]:
                size = tables[h].shape[0]
                begin = out_refs[h][0].shape[0] - 3 * size
                for i, part in enumerate(in_three(tables[h][...])):
                    out_refs[h][0][begin + i * size : begin + (i + 1) * size] = part
        if copies_pool:
            pltpu.make_async_copy(pool_refs[0], new_pool, sem).wait()


def attend(info, queries, sources, packed, scale, group, page=None, prev=None, pool=None):
    halves = len(queries)
    rows = queries[0].shape[0]
    size = 2 * (rows // block_rows)
    step_rows = min(rows, 512 // halves)
    key_count = sum(s.shape[0] * s.shape[2] for s in sources)
    by_rows = pl.BlockSpec((step_rows, lanes), lambda i, *_: (i, 0))
    anywhere = pl.BlockSpec(memory_space=pl.ANY)
    args = list(queries) + list(sources)
    in_specs = [by_rows] * halves + [whole(s) for s in sources]
    if page is not None:
        args.append(page)
        in_specs.append(whole(page))
        key_count += page.shape[1]
    if prev is not None:
        for mixed, table in prev:
            args += [mixed, table]
            in_specs += [by_rows, whole(table)]
    if pool is not None:
        args += list(pool)
        in_specs += [anywhere, anywhere]
    out_shape = []
    out_specs = []
    scratch = [pltpu.VMEM((key_count, 2 * lanes), jnp.bfloat16)]
    table_spec = pl.BlockSpec((size, lanes), lambda i, *_: (0, 0))
    for h in range(halves):
        if packed[h]:
            full_rows = rows + 3 * size
            out_shape.append(jax.ShapeDtypeStruct((full_rows, lanes), jnp.bfloat16))
            out_specs.append(pl.BlockSpec((full_rows, lanes), lambda i, *_: (0, 0)))
            scratch.append(pltpu.VMEM((size, lanes), jnp.float32))
        else:
            out_shape.append(jax.ShapeDtypeStruct((rows, lanes), jnp.float32))
            out_shape.append(jax.ShapeDtypeStruct((size, lanes), jnp.float32))
            out_specs += [by_rows, table_spec]
    if pool is not None:
        out_shape.append(jax.ShapeDtypeStruct(pool[0].shape, pool[0].dtype))
        out_specs.append(anywhere)
        scratch.append(pltpu.SemaphoreType.DMA)
    flops = 4 * halves * rows * key_count * lanes
    return pl.pallas_call(
        functools.partial(
            attend_body,
            halves=halves,
            source_count=len(sources),
            has_page=page is not None,
            has_prev=prev is not None,
            packed=packed,
            step_rows=step_rows,
            group=group,
            scale=scale,
            copies_pool=pool is not None,
        ),
        out_shape=out_shape,
        grid_spec=pltpu.PrefetchScalarGridSpec(
            num_scalar_prefetch=1,
            grid=(rows // step_rows,),
            in_specs=in_specs,
            out_specs=out_specs,
            scratch_shapes=scratch,
        ),
        cost_estimate=pl.CostEstimate(
            flops=flops, transcendentals=halves * rows * key_count, bytes_accessed=4 * key_count * lanes
        ),
        name="attend",
    )(info, *args)


def join_body(own_mixed, own_table, *refs, scale, packs, aliased):
    refs = list(refs)
    out_ref = refs.pop()
    if aliased:
        refs.pop()
    size = own_table.shape[0]
    count = size // 2
    rows = count * block_rows
    eye = diagonal()
    tops = [own_table[:count]]
    totals = [own_table[count:]]
    for ref in refs:
        table = from_three(ref, rows, size)
        tops.append(table[:count])
        totals.append(table[count:])
    top = functools.reduce(jnp.maximum, tops)
    keeps = [jnp.exp2((t - top) * scale) for t in tops]
    total = sum(t * keep for t, keep in zip(totals, keeps))
    if not packs:
        keeps = [keep / total for keep in keeps]
    for t in range(count):
        at = slice(t * block_rows, (t + 1) * block_rows)
        mixed = own_mixed[at] * as_column(keeps[0][t : t + 1], eye)
        for ref, keep in zip(refs, keeps[1:]):
            mixed = mixed + ref[at].astype(jnp.float32) * as_column(keep[t : t + 1], eye)
        if packs:
            out_ref[at] = mixed.astype(jnp.bfloat16)
        else:
            heads = out_ref.shape[1]
            tokens = block_rows // heads
            shaped = mixed.reshape(tokens, heads, lanes)
            out_ref[t * tokens : (t + 1) * tokens] = shaped.astype(jnp.bfloat16)
    if packs:
        table = jnp.concatenate([top, total], axis=0)
        for i, part in enumerate(in_three(table)):
            out_ref[rows + i * size : rows + (i + 1) * size] = part


def join_packed(own, received, scale):
    mixed, table = own
    return pl.pallas_call(
        functools.partial(join_body, scale=scale, packs=True, aliased=False),
        out_shape=jax.ShapeDtypeStruct(received.shape, received.dtype),
        grid=(1,),
        in_specs=[whole(mixed), whole(table), whole(received)],
        out_specs=whole(received),
        name="join_packed",
    )(mixed, table, received)


def join_out(own, received, target, shape, index, group, scale):
    mixed, table = own
    args = [mixed, table, *received]
    in_specs = [whole(a) for a in args]
    aliases = {}
    if target is not None:
        aliases = {len(args): 0}
        args.append(target)
        in_specs.append(pl.BlockSpec(memory_space=pl.ANY))
    return pl.pallas_call(
        functools.partial(join_body, scale=scale, packs=False, aliased=target is not None),
        out_shape=jax.ShapeDtypeStruct(shape, jnp.bfloat16),
        grid=(1,),
        in_specs=in_specs,
        out_specs=pl.BlockSpec((shape[0], group, shape[2]), lambda i: (0, index, 0)),
        input_output_aliases=aliases,
        name="join_out",
    )(*args)


def visible_counts(table, lengths, owner, steps, slot_count, page_len):
    requests, width = table.shape
    pair = owner // 2
    holders = owner ^ (2 * jnp.arange(steps, dtype=jnp.int32))
    chosen = pair ^ (jnp.arange(2, dtype=jnp.int32) * steps)
    column = jnp.arange(width, dtype=jnp.int32)
    count = jnp.clip(lengths[:, None] - column[None, :] * page_len, 0, page_len)
    first = holders[None, :, None, None] * slot_count
    entry = table[None, None]
    held = (entry >= first) & (entry < first + slot_count)
    asked = jnp.arange(requests, dtype=jnp.int32)[None, :] == chosen[:, None]
    picked = held & asked[:, None, :, None]
    return jnp.sum(jnp.where(picked, count[None, None], 0), axis=(2, 3))


def on_device(queries, new_kv, pool, block_table, prefix_len, new_slots):
    owner_count = lax.axis_size("pool")
    owner = lax.axis_index("pool").astype(jnp.int32)
    half = 1 - ((owner % 2) ^ (owner // 2 % 2))
    slot_count, _, kv_heads, page_len, head_dim = pool.shape
    tokens, q_heads, _ = queries.shape
    group = q_heads // kv_heads
    rows = tokens * group
    pairs = owner_count // 2
    near = pairs // 2
    cap = block_table.shape[1] // owner_count
    scale = head_dim**-0.5 * log2_e

    split = [
        queries[:, k * group : (k + 1) * group].reshape(rows, head_dim) for k in range(kv_heads)
    ]
    far_own = [moved(q, pairs) for q in split]
    other = [moved(q, 1) for q in split]
    owner_list = jnp.full((1,), owner, jnp.int32)
    sent_far = gather_pages(owner_list, block_table, pool, [near + k for k in range(1, near)], cap)
    got_far = [
        [moved(sent_far[i][k], 2 * (i + 1)) for i in range(near - 1)] for k in range(kv_heads)
    ]
    kept = gather_pages(owner_list, block_table, pool, [0, near] + list(range(1, near)), cap)
    local, local_far, sent_near = kept[0], kept[1], kept[2:]
    got_near = [
        [moved(sent_near[i][k], 2 * (i + 1)) for i in range(near - 1)] for k in range(kv_heads)
    ]
    seen = visible_counts(block_table, prefix_len, owner, near, slot_count, page_len)
    own_slot = lax.dynamic_index_in_dim(new_slots, owner, 0, keepdims=False) - owner * slot_count
    page_seen = jnp.where(half == 0, page_len, 0)
    new_page = new_kv.transpose(1, 2, 0, 3)
    local_info = jnp.concatenate([seen[0, :1], jnp.stack([page_seen, own_slot])]).astype(jnp.int32)

    started = []
    updated = None
    for k in range(kv_heads):
        results = attend(
            local_info,
            [split[k], other[k]],
            [local[k]],
            (False, False),
            scale,
            group,
            page=new_page[:, k],
            pool=(pool, new_page) if k == 0 else None,
        )
        if k == 0:
            updated = results[4]
        started.append(((results[0], results[1]), (results[2], results[3])))

    far_other = [moved(q, 1) for q in far_own]
    back = []
    for k in range(kv_heads):
        keys = [local_far[k]] + got_far[k]
        own_far = attend(seen[1], [far_own[k]], keys, (False,), scale, group)
        (other_far,) = attend(seen[1], [far_other[k]], keys, (True,), scale, group)
        joined = join_packed(own_far, moved(other_far, 1), scale)
        back.append(moved(joined, pairs))
    attended = None
    for k in range(kv_heads):
        mine, theirs = started[k]
        (other_part,) = attend(seen[0, 1:], [other[k]], got_near[k], (True,), scale, group, prev=[theirs])
        own_part = attend(seen[0, 1:], [split[k]], got_near[k], (False,), scale, group, prev=[mine])
        attended = join_out(
            own_part, [moved(other_part, 1), back[k]], attended, queries.shape, k, group, scale
        )
    return (attended, updated)


def solution(mesh):
    placed = (
        P(("groups", "pool"), "head", None),
        P(("groups", "pool"), None, "head", None),
        P(("groups", "pool"), None, "head", None, None),
        P("groups", None),
        P("groups"),
        P("groups"),
    )
    return jax.shard_map(
        on_device,
        mesh=mesh,
        in_specs=placed,
        out_specs=(
            P(("groups", "pool"), "head", None),
            P(("groups", "pool"), None, "head", None, None),
        ),
        check_vma=False,
    )
```

time: 200 us -> 370 us (1.85)
  Pallas kernels: 0 us -> 332 us
  waiting for transfers between devices: 92.7 us -> 4.27 us
  matrix products: 38.2 us -> 0 us
  local copies, waits for them, and re-layouts: 31 us -> 10.4 us
  other arithmetic: 22.3 us -> 1.74 us
  starting transfers between devices: 13.2 us -> 19.5 us
    pallas_call x0 -> x16, Pallas kernels: none -> 332 us  [the longest x10 190 us: attend(): pl.pallas_call(functools.partial(attend_body, halves=halves, source_count...]
    ppermute x5 -> x16, waiting for transfers between devices: 54.8 us -> 4.27 us  [moved(): return lax.ppermute(array, 'pool', [(i, i ^ apart) for i in range(count)])]
    dot_general x10 -> x0, matrix products: 38.2 us -> none  [the longest x4 25.7 us: carry_values(): jnp.einsum('kgtnp,nkpd->kgtd', shaped, page_block[:, 1], preferred_elemen...]
    all_to_all x1 -> x0, waiting for transfers between devices: 37.9 us -> none  [on_device(): lax.all_to_all(buffer, 'pool', split_axis=0, concat_axis=0, tiled=True)]
    reduce_sum x7 -> x1, other arithmetic: 19.2 us -> 0.23 us  [visible_counts(): return jnp.sum(jnp.where(picked, count[None, None], 0), axis=(2, 3))]
    ppermute x5 -> x16, starting transfers between devices: 5.79 us -> 19.5 us  [moved(): return lax.ppermute(array, 'pool', [(i, i ^ apart) for i in range(count)])]
    gather x4 -> x0, local copies, waits for them, and re-layouts: 11.2 us -> none  [the longest x2 9.98 us: prepare(): buffer = pool[send_slots]]
    all_to_all x1 -> x0, starting transfers between devices: 7.44 us -> none  [on_device(): lax.all_to_all(buffer, 'pool', split_axis=0, concat_axis=0, tiled=True)]
  transfers between devices with their start and end apart: 6 -> 16, of which waited for: 4 -> 2; matrix products, arithmetic and copies ran while one was open for 4% -> 1% of each run, Pallas kernels for 0% -> 89%
where the time goes in v1:
time: 370 us; the launch traced here: 369 us
  Pallas kernels  332 us (90%)
  starting transfers between devices  19.5 us (5%)
  local copies, waits for them, and re-layouts  10.4 us (3%)
  waiting for transfers between devices  4.27 us (1%)
    pallas_call x10, Pallas kernels, attend(): pl.pallas_call(functools.partial(attend_body, halves=halves, source_count...  190 us
    pallas_call x2, Pallas kernels, gather_pages(): pl.pallas_call(functools.partial(gather_body, lists=lists, kv_heads=kv_he...  132 us
    ppermute x16, starting transfers between devices, moved(): return lax.ppermute(array, 'pool', [(i, i ^ apart) for i in range(count)])  19.5 us
  transfers between devices with their start and end apart: 16, of which 2 were waited for; matrix products, arithmetic and copies ran while one was open for 1% of the time, Pallas kernels for 89%

profile of v1, /device:TPU:0, one launch (start us, length us, event | category | flops | bytes accessed | tf_op | source)
XLA Modules:
  0.0 369.3 jit_solution(9291548824872429512)
XLA Ops:
  0.7 1.1 slice_bitcast_fusion
  1.8 4.1 %collective-permute-start.11 = (bf16[1024,128]{1,0:T(8,128)(2,1)S(1)}, bf16[1024,128]{1,0:T(8,128)(2,1)S(1)}, u32[]{:S(2)}, u32[]{:S(2)}) collective-permute-start(bf16[1024,128]{1,0:T(8,128)(2,1)S(1)} %get-tuple-element.52.refs_0_), channel_id=1, source_target_pairs={{0,8},{2,10},{4,12},{6,14},{8,0},{10,2},{12,4},{14,6},{1,9},{3,11}... | collective-permute-start | bytes 786440 | tf_op jit(solution)/shard_map/ppermute | solution.py:19
  5.9 1.5 collective-permute-start.9
  7.4 0.3 collective-permute-start.3
  7.8 0.2 collective-permute-start.1
  8.0 34.2 %gather_pages.3 = (bf16[8,2,128,128]{3,2,1,0:T(8,128)(2,1)}, bf16[8,2,128,128]{3,2,1,0:T(8,128)(2,1)}) custom-call(s32[1]{0:T(128)} %bitcast.2.owner_ref, s32[4,64]{1,0:T(4,128)} %table_ref.3, bf16[33,2,2,128,128]{4,3,2,1,0:T(8,128)(2,1)} %refs_4_.1), custom_call_target="tpu_custom_call" | custom-call | tf_op jit(solution)/shard_map/gather_pages/pallas_call | solution.py:92
  42.2 1.9 collective-permute-start.12
  44.2 0.7 slice_bitcast_fusion.2
  45.4 1.6 collective-permute-start.13
  47.0 0.6 slice_bitcast_fusion.4.info_ref
  47.5 97.9 %gather_pages.2 = (bf16[8,2,128,128]{3,2,1,0:T(8,128)(2,1)}, bf16[8,2,128,128]{3,2,1,0:T(8,128)(2,1)}, bf16[8,2,128,128]{3,2,1,0:T(8,128)(2,1)}, bf16[8,2,128,12...) custom-call(s32[1]{0:T(128)} %bitcast.2.owner_ref, s32[4,64]{1,0:T(4,128)} %table_ref.3, ...), custom_call_target="tpu_custom_call" | custom-call | tf_op jit(solution)/shard_map/gather_pages/pallas_call | solution.py:92
  145.5 0.7 dynamic_slice.4
  146.8 0.5 collective-permute-start.4
  147.3 0.6 fusion.1
  148.0 1.6 collective-permute-start
  149.5 0.7 copy-done.19
  150.3 0.4 collective-permute-start.8
  150.7 1.3 pad_add_fusion.info_ref
  152.0 0.2 collective-permute-start.5
  152.3 8.1 %attend.10 = (f32[1024,128]{1,0:T(8,128)}, f32[16,128]{1,0:T(8,128)}, f32[1024,128]{1,0:T(8,128)}, f32[16,128]{1,0:T(8,128)}) custom-call(s32[3]{0:T(128)} %pad_add_fusion.info_ref, bf16[1024,128]{1,0:T(8,128)(2,1)} %copy-done.9, bf16[1024,128]{1,0:T(8,128)(2,1)} %copy-done.19, bf16[8,2,128,128]{3,2,1,0:T(8,128)(2,1)} %get-tuple-element.28.refs_2_, ...), custom_call_target="tpu_custom_call" | custom-call | flops 1207959552 | bytes 589824 | tf_op jit(solution)/shard_map/attend/pallas_call | solution.py:279
  160.4 134.7 %attend.15 = (f32[1024,128]{1,0:T(8,128)}, f32[16,128]{1,0:T(8,128)}, f32[1024,128]{1,0:T(8,128)}, f32[16,128]{1,0:T(8,128)}, bf16[33,2,2,128,128]{4,3,2,1,0:T(8,128)(2,1)}) custom-call(s32[3]{0:T(128)} %pad_add_fusion.info_ref, bf16[1024,128]{1,0:T(8,128)(2,1)} %copy-done.1, bf16[1024,128]{1,0:T(8,128)(2,1)} %copy-done.8, ...), custom_call_target="tpu_custom_call" | custom-call | flops 1207959552 | bytes 589824 | tf_op jit(solution)/shard_map/attend/pallas_call | solution.py:279
  295.1 0.8 copy-done.13
  295.9 6.7 %attend.19 = bf16[1072,128]{1,0:T(8,128)(2,1)} custom-call(s32[2]{0:T(128)} %slice_bitcast_fusion.4.info_ref, bf16[1024,128]{1,0:T(8,128)(2,1)} %collective-permute-done.13.refs_0_, bf16[8,2,128,128]{3,2,1,0:T(8,128)(2,1)} %get-tuple-element.47.refs_1_, bf16[8,2,128,128]{3,2,1,0:T(8,128)(2,1)} %copy-done.13), custom_call_target="tpu_custom_call" | custom-call | flops 1073741824 | bytes 1048576 | tf_op jit(solution)/shard_map/attend/pallas_call | solution.py:279
  302.7 1.8 collective-permute-start.14
  304.4 0.7 copy-done.20
  305.1 6.8 %attend.14 = bf16[1072,128]{1,0:T(8,128)(2,1)} custom-call(s32[2]{0:T(128)} %slice_bitcast_fusion.4.info_ref, bf16[1024,128]{1,0:T(8,128)(2,1)} %copy-done.20, bf16[8,2,128,128]{3,2,1,0:T(8,128)(2,1)} %get-tuple-element.35.refs_1_, bf16[8,2,128,128]{3,2,1,0:T(8,128)(2,1)} %collective-permute-done.4.refs_2_), custom_call_target="tpu_custom_call" | custom-call | flops 1073741824 | bytes 1048576 | tf_op jit(solution)/shard_map/attend/pallas_call | solution.py:279
  311.9 0.3 collective-permute-start.6
  312.2 0.8 copy-done.16
  312.9 5.3 %attend.12 = bf16[1072,128]{1,0:T(8,128)(2,1)} custom-call(s32[1]{0:T(128)} %bitcast.info_ref, bf16[1024,128]{1,0:T(8,128)(2,1)} %copy-done.19, bf16[8,2,128,128]{3,2,1,0:T(8,128)(2,1)} %copy-done.16, f32[1024,128]{1,0:T(8,128)} %get-tuple-element.33.refs_2_, f32[16,128]{1,0:T(8,128)} %get-tuple-element.34.refs_3_), custom_call_target="tpu_custom_call" | custom-call | flops 536870912 | bytes 524288 | tf_op jit(solution)/shard_map/attend/pallas_call | solution.py:279
  318.2 1.8 collective-permute-start.2
  320.0 0.8 copy-done.15
  320.8 5.2 %attend.17 = bf16[1072,128]{1,0:T(8,128)(2,1)} custom-call(s32[1]{0:T(128)} %bitcast.info_ref, bf16[1024,128]{1,0:T(8,128)(2,1)} %copy-done.8, bf16[8,2,128,128]{3,2,1,0:T(8,128)(2,1)} %copy-done.15, f32[1024,128]{1,0:T(8,128)} %get-tuple-element.45.refs_2_, f32[16,128]{1,0:T(8,128)} %get-tuple-element.46.refs_3_), custom_call_target="tpu_custom_call" | custom-call | flops 536870912 | bytes 524288 | tf_op jit(solution)/shard_map/attend/pallas_call | solution.py:279
  326.0 0.2 collective-permute-start.10
  326.3 6.8 %attend.13 = (f32[1024,128]{1,0:T(8,128)}, f32[16,128]{1,0:T(8,128)}) custom-call(s32[2]{0:T(128)} %slice_bitcast_fusion.4.info_ref, bf16[1024,128]{1,0:T(8,128)(2,1)} %copy-done.18, bf16[8,2,128,128]{3,2,1,0:T(8,128)(2,1)} %get-tuple-element.35.refs_1_, bf16[8,2,128,128]{3,2,1,0:T(8,128)(2,1)} %collective-permute-done.4.refs_2_), custom_call_target="tpu_custom_call" | custom-call | flops 1073741824 | bytes 1048576 | tf_op jit(solution)/shard_map/attend/pallas_call | solution.py:279
  333.1 6.7 %attend.18 = (f32[1024,128]{1,0:T(8,128)}, f32[16,128]{1,0:T(8,128)}) custom-call(s32[2]{0:T(128)} %slice_bitcast_fusion.4.info_ref, bf16[1024,128]{1,0:T(8,128)(2,1)} %copy-done.17, bf16[8,2,128,128]{3,2,1,0:T(8,128)(2,1)} %get-tuple-element.47.refs_1_, bf16[8,2,128,128]{3,2,1,0:T(8,128)(2,1)} %copy-done.13), custom_call_target="tpu_custom_call" | custom-call | flops 1073741824 | bytes 1048576 | tf_op jit(solution)/shard_map/attend/pallas_call | solution.py:279
  339.8 0.7 copy-done.4
  340.5 2.2 join_packed.3
  342.7 2.8 collective-permute-start.15
  345.6 0.7 copy-done.5
  346.3 2.2 join_packed.2
  348.6 5.1 %attend.11 = (f32[1024,128]{1,0:T(8,128)}, f32[16,128]{1,0:T(8,128)}) custom-call(s32[1]{0:T(128)} %bitcast.info_ref, bf16[1024,128]{1,0:T(8,128)(2,1)} %copy-done.9, bf16[8,2,128,128]{3,2,1,0:T(8,128)(2,1)} %copy-done.16, f32[1024,128]{1,0:T(8,128)} %get-tuple-element.29.refs_2_, f32[16,128]{1,0:T(8,128)} %get-tuple-element.30.refs_3_), custom_call_target="tpu_custom_call" | custom-call | flops 536870912 | bytes 524288 | tf_op jit(solution)/shard_map/attend/pallas_call | solution.py:279
  353.7 5.1 %attend.16 = (f32[1024,128]{1,0:T(8,128)}, f32[16,128]{1,0:T(8,128)}) custom-call(s32[1]{0:T(128)} %bitcast.info_ref, bf16[1024,128]{1,0:T(8,128)(2,1)} %copy-done.1, bf16[8,2,128,128]{3,2,1,0:T(8,128)(2,1)} %copy-done.15, f32[1024,128]{1,0:T(8,128)} %get-tuple-element.41.refs_2_, f32[16,128]{1,0:T(8,128)} %get-tuple-element.42.refs_3_), custom_call_target="tpu_custom_call" | custom-call | flops 536870912 | bytes 524288 | tf_op jit(solution)/shard_map/attend/pallas_call | solution.py:279
  358.8 3.3 collective-permute-done.15.refs_1_
  362.1 0.7 copy-done.3
  362.8 2.4 join_out.2.refs_2_
  365.2 0.9 collective-permute-done.7.refs_1_
  366.2 0.7 copy-done.7
  366.9 2.4 join_out.3
  (58 shorter events, 0.7 us)
Async XLA Ops:
  0.6 44.3 %copy-start.11 = (s32[4,64]{1,0:T(4,128)S(1)}, s32[4,64]{1,0:T(4,128)}, u32[]{:S(2)}) copy-start(s32[4,64]{1,0:T(4,128)} %table_ref.3) | copy-start | bytes 3076
  0.6 43.5 %copy-start.10 = (bf16[128,2,2,128]{3,2,1,0:T(2,128)(2,1)S(1)}, bf16[128,2,2,128]{3,2,1,0:T(2,128)(2,1)}, u32[]{:S(2)}) copy-start(bf16[128,2,2,128]{3,2,1,0:T(2,128)(2,1)} %param.7) | copy-start | bytes 393220
  0.7 44.3 %copy-start.12 = (s32[4]{0:T(128)S(1)}, s32[4]{0:T(128)}, u32[]{:S(2)}) copy-start(s32[4]{0:T(128)} %param.10) | copy-start | bytes 52
  1.8 143.6 %copy-start.1 = (bf16[1024,128]{1,0:T(8,128)(2,1)}, bf16[1024,128]{1,0:T(8,128)(2,1)S(1)}, u32[]{:S(2)}) copy-start(bf16[1024,128]{1,0:T(8,128)(2,1)S(1)} %get-tuple-element.52.refs_0_) | copy-start | bytes 786436
  1.8 143.6 %copy-start.9 = (bf16[1024,128]{1,0:T(8,128)(2,1)}, bf16[1024,128]{1,0:T(8,128)(2,1)S(1)}, u32[]{:S(2)}) copy-start(bf16[1024,128]{1,0:T(8,128)(2,1)S(1)} %get-tuple-element.53.refs_0_) | copy-start | bytes 786436
  1.8 43.6 %collective-permute-start.11 = (bf16[1024,128]{1,0:T(8,128)(2,1)S(1)}, bf16[1024,128]{1,0:T(8,128)(2,1)S(1)}, u32[]{:S(2)}, u32[]{:S(2)}) collective-permute-start(bf16[1024,128]{1,0:T(8,128)(2,1)S(1)} %get-tuple-element.52.refs_0_), channel_id=1, source_target_pairs={{0,8},{2,10},{4,12},{6,14},{8,0},{10,2},{12,4},{14,6},{1,9},{3,11}... | collective-permute-start | bytes 786440 | tf_op jit(solution)/shard_map/ppermute | solution.py:19
  5.9 140.9 %collective-permute-start.9 = (bf16[1024,128]{1,0:T(8,128)(2,1)S(1)}, bf16[1024,128]{1,0:T(8,128)(2,1)S(1)}, u32[]{:S(2)}, u32[]{:S(2)}) collective-permute-start(bf16[1024,128]{1,0:T(8,128)(2,1)S(1)} %get-tuple-element.52.refs_0_), channel_id=1, source_target_pairs={{0,2},{2,0},{4,6},{6,4},{8,10},{10,8},{12,14},{14,12},{1,3},{3,1},... | collective-permute-start | bytes 786440 | tf_op jit(solution)/shard_map/ppermute | solution.py:19
  7.4 140.5 %collective-permute-start.3 = (bf16[1024,128]{1,0:T(8,128)(2,1)S(1)}, bf16[1024,128]{1,0:T(8,128)(2,1)S(1)}, u32[]{:S(2)}, u32[]{:S(2)}) collective-permute-start(bf16[1024,128]{1,0:T(8,128)(2,1)S(1)} %get-tuple-element.53.refs_0_), channel_id=1, source_target_pairs={{0,8},{2,10},{4,12},{6,14},{8,0},{10,2},{12,4},{14,6},{1,9},{3,11}... | collective-permute-start | bytes 786440 | tf_op jit(solution)/shard_map/ppermute | solution.py:19
  7.8 141.8 %collective-permute-start.1 = (bf16[1024,128]{1,0:T(8,128)(2,1)S(1)}, bf16[1024,128]{1,0:T(8,128)(2,1)S(1)}, u32[]{:S(2)}, u32[]{:S(2)}) collective-permute-start(bf16[1024,128]{1,0:T(8,128)(2,1)S(1)} %get-tuple-element.53.refs_0_), channel_id=1, source_target_pairs={{0,2},{2,0},{4,6},{6,4},{8,10},{10,8},{12,14},{14,12},{1,3},{3,1},... | collective-permute-start | bytes 786440 | tf_op jit(solution)/shard_map/ppermute | solution.py:19
  8.0 137.4 %copy-start.21 = (s32[8]{0:T(128)S(1)}, s32[8]{0:T(128)}, u32[]{:S(2)}) copy-start(s32[8]{0:T(128)} %param.11) | copy-start | bytes 100
  42.2 104.6 %copy-start.14 = (bf16[8,2,128,128]{3,2,1,0:T(8,128)(2,1)S(1)}, bf16[8,2,128,128]{3,2,1,0:T(8,128)(2,1)}, u32[]{:S(2)}) copy-start(bf16[8,2,128,128]{3,2,1,0:T(8,128)(2,1)} %get-tuple-element.36) | copy-start | bytes 1572868
  42.2 252.9 %collective-permute-start.12 = (bf16[8,2,128,128]{3,2,1,0:T(8,128)(2,1)}, bf16[8,2,128,128]{3,2,1,0:T(8,128)(2,1)S(1)}, u32[]{:S(2)}, u32[]{:S(2)}) collective-permute-start(bf16[8,2,128,128]{3,2,1,0:T(8,128)(2,1)} %get-tuple-element.48), channel_id=1, source_target_pairs={{0,4},{2,6},{4,0},{6,2},{8,12},{10,14},{12,8},{14,10},{1,5},{3,7},... | collective-permute-start | bytes 1572872 | tf_op jit(solution)/shard_map/ppermute | solution.py:19
  44.2 116.2 %copy-start = (bf16[128,2,2,128]{3,0,2,1:T(8,128)(2,1)}, bf16[128,2,2,128]{3,0,2,1:T(8,128)(2,1)S(1)}, u32[]{:S(2)}) copy-start(bf16[128,2,2,128]{3,0,2,1:T(8,128)(2,1)S(1)} %copy.12) | copy-start | bytes 393220
  45.4 115.1 %copy-start.17 = (bf16[1024,128]{1,0:T(8,128)(2,1)}, bf16[1024,128]{1,0:T(8,128)(2,1)S(1)}, u32[]{:S(2)}) copy-start(bf16[1024,128]{1,0:T(8,128)(2,1)S(1)} %collective-permute-done.11.refs_0_) | copy-start | bytes 786436
  45.4 106.6 %collective-permute-start.13 = (bf16[1024,128]{1,0:T(8,128)(2,1)S(1)}, bf16[1024,128]{1,0:T(8,128)(2,1)}, u32[]{:S(2)}, u32[]{:S(2)}) collective-permute-start(bf16[1024,128]{1,0:T(8,128)(2,1)S(1)} %collective-permute-done.11.refs_0_), channel_id=1, source_target_pairs={{0,2},{2,0},{4,6},{6,4},{8,10},{10,8},{12,14},{14,12},{1,3},{3,1},... | collective-permute-start | bytes 786440 | tf_op jit(solution)/shard_map/ppermute | solution.py:19
  146.8 13.6 %copy-start.8 = (bf16[1024,128]{1,0:T(8,128)(2,1)}, bf16[1024,128]{1,0:T(8,128)(2,1)S(1)}, u32[]{:S(2)}) copy-start(bf16[1024,128]{1,0:T(8,128)(2,1)S(1)} %collective-permute-done.9.refs_1_.refs_0_) | copy-start | bytes 786436
  146.8 157.6 %collective-permute-start.4 = (bf16[8,2,128,128]{3,2,1,0:T(8,128)(2,1)S(1)}, bf16[8,2,128,128]{3,2,1,0:T(8,128)(2,1)}, u32[]{:S(2)}, u32[]{:S(2)}) collective-permute-start(bf16[8,2,128,128]{3,2,1,0:T(8,128)(2,1)S(1)} %copy-done.14), channel_id=1, source_target_pairs={{0,4},{2,6},{4,0},{6,2},{8,12},{10,14},{12,8},{14,10},{1,5},{3,7},... | collective-permute-start | bytes 1572872 | tf_op jit(solution)/shard_map/ppermute | solution.py:19
  148.0 147.2 %copy-start.18 = (bf16[1024,128]{1,0:T(8,128)(2,1)}, bf16[1024,128]{1,0:T(8,128)(2,1)S(1)}, u32[]{:S(2)}) copy-start(bf16[1024,128]{1,0:T(8,128)(2,1)S(1)} %collective-permute-done.3.refs_0_) | copy-start | bytes 786436
  148.0 164.2 %collective-permute-start = (bf16[8,2,128,128]{3,2,1,0:T(8,128)(2,1)}, bf16[8,2,128,128]{3,2,1,0:T(8,128)(2,1)S(1)}, u32[]{:S(2)}, u32[]{:S(2)}) collective-permute-start(bf16[8,2,128,128]{3,2,1,0:T(8,128)(2,1)} %get-tuple-element.27), channel_id=1, source_target_pairs={{0,4},{2,6},{4,0},{6,2},{8,12},{10,14},{12,8},{14,10},{1,5},{3,7},... | collective-permute-start | bytes 1572872 | tf_op jit(solution)/shard_map/ppermute | solution.py:19
  149.5 0.7 copy-start.19
  150.3 169.7 %collective-permute-start.8 = (bf16[8,2,128,128]{3,2,1,0:T(8,128)(2,1)}, bf16[8,2,128,128]{3,2,1,0:T(8,128)(2,1)S(1)}, u32[]{:S(2)}, u32[]{:S(2)}) collective-permute-start(bf16[8,2,128,128]{3,2,1,0:T(8,128)(2,1)} %get-tuple-element.39), channel_id=1, source_target_pairs={{0,4},{2,6},{4,0},{6,2},{8,12},{10,14},{12,8},{14,10},{1,5},{3,7},... | collective-permute-start | bytes 1572872 | tf_op jit(solution)/shard_map/ppermute | solution.py:19
  152.0 152.4 %collective-permute-start.5 = (bf16[1024,128]{1,0:T(8,128)(2,1)S(1)}, bf16[1024,128]{1,0:T(8,128)(2,1)S(1)}, u32[]{:S(2)}, u32[]{:S(2)}) collective-permute-start(bf16[1024,128]{1,0:T(8,128)(2,1)S(1)} %collective-permute-done.3.refs_0_), channel_id=1, source_target_pairs={{0,2},{2,0},{4,6},{6,4},{8,10},{10,8},{12,14},{14,12},{1,3},{3,1},... | collective-permute-start | bytes 786440 | tf_op jit(solution)/shard_map/ppermute | solution.py:19
  295.1 0.8 copy-start.13
  302.7 37.1 %collective-permute-start.14 = (bf16[1072,128]{1,0:T(8,128)(2,1)}, bf16[1072,128]{1,0:T(8,128)(2,1)S(1)}, u32[]{:S(2)}, u32[]{:S(2)}) collective-permute-start(bf16[1072,128]{1,0:T(8,128)(2,1)} %attend.19), channel_id=1, source_target_pairs={{0,2},{2,0},{4,6},{6,4},{8,10},{10,8},{12,14},{14,12},{1,3},{3,1},... | collective-permute-start | bytes 823304 | tf_op jit(solution)/shard_map/ppermute | solution.py:19
  304.4 0.7 copy-start.20
  311.9 33.7 %collective-permute-start.6 = (bf16[1072,128]{1,0:T(8,128)(2,1)}, bf16[1072,128]{1,0:T(8,128)(2,1)S(1)}, u32[]{:S(2)}, u32[]{:S(2)}) collective-permute-start(bf16[1072,128]{1,0:T(8,128)(2,1)} %attend.14), channel_id=1, source_target_pairs={{0,2},{2,0},{4,6},{6,4},{8,10},{10,8},{12,14},{14,12},{1,3},{3,1},... | collective-permute-start | bytes 823304 | tf_op jit(solution)/shard_map/ppermute | solution.py:19
  312.2 0.8 copy-start.16
  318.2 47.0 %collective-permute-start.2 = (bf16[1072,128]{1,0:T(8,128)(2,1)}, bf16[1072,128]{1,0:T(8,128)(2,1)S(1)}, u32[]{:S(2)}, u32[]{:S(2)}) collective-permute-start(bf16[1072,128]{1,0:T(8,128)(2,1)} %attend.12), channel_id=1, source_target_pairs={{0,2},{2,0},{4,6},{6,4},{8,10},{10,8},{12,14},{14,12},{1,3},{3,1},... | collective-permute-start | bytes 823304 | tf_op jit(solution)/shard_map/ppermute | solution.py:19
  320.0 0.8 copy-start.15
  326.0 32.7 %collective-permute-start.10 = (bf16[1072,128]{1,0:T(8,128)(2,1)}, bf16[1072,128]{1,0:T(8,128)(2,1)S(1)}, u32[]{:S(2)}, u32[]{:S(2)}) collective-permute-start(bf16[1072,128]{1,0:T(8,128)(2,1)} %attend.17), channel_id=1, source_target_pairs={{0,2},{2,0},{4,6},{6,4},{8,10},{10,8},{12,14},{14,12},{1,3},{3,1},... | collective-permute-start | bytes 823304 | tf_op jit(solution)/shard_map/ppermute | solution.py:19
  339.8 0.7 copy-start.4
  342.7 19.4 %collective-permute-start.15 = (bf16[1072,128]{1,0:T(8,128)(2,1)}, bf16[1072,128]{1,0:T(8,128)(2,1)S(1)}, u32[]{:S(2)}, u32[]{:S(2)}) collective-permute-start(bf16[1072,128]{1,0:T(8,128)(2,1)} %join_packed.3), channel_id=1, source_target_pairs={{0,8},{2,10},{4,12},{6,14},{8,0},{10,2},{12,4},{14,6},{1,9},{3,11}... | collective-permute-start | bytes 823304 | tf_op jit(solution)/shard_map/ppermute | solution.py:19
  345.6 0.7 copy-start.5
  348.5 17.7 %collective-permute-start.7 = (bf16[1072,128]{1,0:T(8,128)(2,1)}, bf16[1072,128]{1,0:T(8,128)(2,1)S(1)}, u32[]{:S(2)}, u32[]{:S(2)}) collective-permute-start(bf16[1072,128]{1,0:T(8,128)(2,1)} %join_packed.2), channel_id=1, source_target_pairs={{0,8},{2,10},{4,12},{6,14},{8,0},{10,2},{12,4},{14,6},{1,9},{3,11}... | collective-permute-start | bytes 823304 | tf_op jit(solution)/shard_map/ppermute | solution.py:19
  358.8 3.3 copy-start.2
  362.1 0.7 copy-start.3
  365.2 0.9 copy-start.6
  366.2 0.7 copy-start.7
